TPU v7x, 32 devices: a whole 2x2x4 slice. The times are simulated.
32 devices in a mesh: batch: 8 (over z, x), seq: 4 (over y, core).
Axes of the slice: x: 2, y: 2, z: 4, core: 2. Of those that a mesh axis runs over, the one named last changes fastest.
Arguments:
- tokens: bfloat16 [8, 1024, 1024], P('batch', 'seq'), may hold values from -6 to 6
- cotangent: bfloat16 [8, 1024, 1024], P('batch', 'seq'), may hold values from -6 to 6
- image_tokens: bfloat16 [8, 1025, 768], P('batch'), may hold values from -6 to 6
- image_lengths: int32 [8], P('batch'), may hold values from 512 to 1025, as said below
- key_mask: int32 [8, 1025], P('batch'), may hold values 0 or 1
- camera: bfloat16 [8, 1024], P(None, 'batch'), may hold values from -6 to 6
- modulation: bfloat16 [1024, 6144], P('batch'), may hold values from -0.1875 to 0.1875
- q_cross: bfloat16 [1024, 1024], P('batch'), may hold values from -0.1875 to 0.1875
- kv_image: bfloat16 [768, 2048], P('batch'), may hold values from -0.21875 to 0.21875
- out_cross: bfloat16 [1024, 1024], P('batch'), may hold values from -3.5 to 3.5
- qkv_self: bfloat16 [1024, 3072], P('batch'), may hold values from -0.1875 to 0.1875
- out_self: bfloat16 [1024, 1024], P('batch'), may hold values from -6 to 6
- mlp_in: bfloat16 [1024, 4096], P('batch'), may hold values from -0.1875 to 0.1875
- mlp_out: bfloat16 [4096, 1024], P('batch'), may hold values from -0.09375 to 0.09375
Outputs:
- output: bfloat16 [8, 1024, 1024], P('batch', 'seq')
- grad_tokens: float32 [8, 1024, 1024], P('batch', 'seq')
- grad_modulation: float32 [1024, 6144], P('batch')
- grad_q_cross: float32 [1024, 1024], P('batch')
- grad_kv_image: float32 [768, 2048], P('batch')
- grad_out_cross: float32 [1024, 1024], P('batch')
- grad_qkv_self: float32 [1024, 3072], P('batch')
- grad_out_self: float32 [1024, 1024], P('batch')
- grad_mlp_in: float32 [1024, 4096], P('batch')
- grad_mlp_out: float32 [4096, 1024], P('batch')
Inputs may be any that keep to these rules, and one draw needn't show every extreme that they name: `image_lengths`: some object has 1025 valid image tokens and some has 512.
All inputs are finite; a program needn't handle non-finite values. No bound on the sum of `key_mask` on one device may be relied on, other than what follows from the above.
Results may differ from a plain program's by a relative error of at most 0.025.
The roundings to bfloat16 on the way count: a program that leaves them out, or rounds other values in their place, can miss the bound.
Values may be sent and summed in bfloat16 or wider, within the bound.
A program may use at most 256 MiB of HBM per device.

v0:
```python
import jax
import jax.numpy as jnp
from jax import lax
from jax.sharding import PartitionSpec as P

HEADS = 16
HEAD_DIM = 64
epsilon = 1e-06
group_heads = 4
highest = lax.Precision.HIGHEST


def modulated_norm(values, shift, scale):
    center = values - jnp.mean(values, axis=-1, keepdims=True)
    normed = center * lax.rsqrt(jnp.mean(center * center, axis=-1, keepdims=True) + epsilon)
    return normed * (1.0 + scale) + shift


def product(left, right):
    return jnp.dot(left, right, preferred_element_type=jnp.float32)


def contract_rows(left, right):
    return lax.dot_general(
        left, right, (((0,), (0,)), ((), ())), preferred_element_type=jnp.float32
    )


def times_transposed(left, right):
    return lax.dot_general(
        left, right, (((1,), (1,)), ((), ())), preferred_element_type=jnp.float32
    )


def split_heads(values):
    rows = values.shape[0]
    grouped = values.reshape(rows, HEADS // group_heads, group_heads, HEAD_DIM)
    return grouped.transpose(1, 2, 0, 3)


def join_heads(values):
    groups, inner, rows, depth = values.shape
    return values.transpose(2, 0, 1, 3).reshape(rows, groups * inner * depth)


def scores_of(query_group, key_group, valid):
    scores = jnp.einsum(
        "hqd,hkd->hqk", query_group, key_group, preferred_element_type=jnp.float32
    ) * HEAD_DIM ** (-0.5)
    return jnp.where(valid[None, None, :], scores, -1000000000.0)


def attend_forward(query, key_rows, value_rows, valid):

    def one_group(pieces):
        query_group, key_group, value_group = pieces
        scores = scores_of(query_group, key_group, valid)
        top = jnp.max(scores, axis=-1, keepdims=True)
        expo = jnp.exp(scores - top)
        total = jnp.sum(expo, axis=-1, keepdims=True)
        probs = (expo / total).astype(jnp.bfloat16)
        result = jnp.einsum("hqk,hkd->hqd", probs, value_group, preferred_element_type=jnp.float32)
        return (result, top, total)

    results, tops, totals = lax.map(
        one_group, (split_heads(query), split_heads(key_rows), split_heads(value_rows))
    )
    return (join_heads(results), (tops, totals))


def attend_backward(query, key_rows, value_rows, valid, stats, grad_output):
    tops, totals = stats

    def one_group(pieces):
        query_group, key_group, value_group, top, total, grad_group = pieces
        scores = scores_of(query_group, key_group, valid)
        probs = jnp.exp(scores - top) / total
        grad_probs = jnp.einsum(
            "hqd,hkd->hqk", grad_group, value_group, preferred_element_type=jnp.float32
        )
        inner = jnp.sum(probs * grad_probs, axis=-1, keepdims=True)
        grad_scores = (probs * (grad_probs - inner)).astype(jnp.bfloat16)
        factor = HEAD_DIM ** (-0.5)
        grad_query = (
            jnp.einsum("hqk,hkd->hqd", grad_scores, key_group, preferred_element_type=jnp.float32)
            * factor
        )
        grad_keys = (
            jnp.einsum("hqk,hqd->hkd", grad_scores, query_group, preferred_element_type=jnp.float32)
            * factor
        )
        grad_values = jnp.einsum(
            "hqk,hqd->hkd",
            probs.astype(jnp.bfloat16),
            grad_group,
            preferred_element_type=jnp.float32,
        )
        return (grad_query, inner, grad_keys, grad_values)

    results = lax.map(
        one_group,
        (
            split_heads(query),
            split_heads(key_rows),
            split_heads(value_rows),
            tops,
            totals,
            split_heads(grad_output),
        ),
    )
    return (join_heads(results[0]), results[1], join_heads(results[2]), join_heads(results[3]))


def local(
    tokens,
    cotangent,
    image_tokens,
    image_lengths,
    key_mask,
    camera,
    modulation,
    q_cross,
    kv_image,
    out_cross,
    qkv_self,
    out_self,
    mlp_in,
    mlp_out,
):
    q_full, kv_full, out_cross_full, qkv_full, out_self_full, mlp_in_full, mlp_out_full = (
        lax.all_gather(q_cross, "batch", axis=0, tiled=True),
        lax.all_gather(kv_image, "batch", axis=0, tiled=True),
        lax.all_gather(out_cross, "batch", axis=0, tiled=True),
        lax.all_gather(qkv_self, "batch", axis=0, tiled=True),
        lax.all_gather(out_self, "batch", axis=0, tiled=True),
        lax.all_gather(mlp_in, "batch", axis=0, tiled=True),
        lax.all_gather(mlp_out, "batch", axis=0, tiled=True),
    )
    camera_gate = jax.nn.silu(camera.astype(jnp.float32)).astype(jnp.bfloat16)
    modulation_all = lax.psum(product(camera_gate, modulation), "batch")
    object_index = lax.axis_index("batch")
    width = tokens.shape[2]
    shifts = lax.dynamic_index_in_dim(modulation_all, object_index, 0, keepdims=False).reshape(
        6, width
    )
    stream = tokens[0].astype(jnp.float32)
    image_rows = image_tokens[0]
    positions = jnp.arange(image_rows.shape[0], dtype=jnp.int32)
    valid = (positions < image_lengths[0]) & ((key_mask[0] == 1) | (positions == 0))
    everywhere = jnp.ones((lax.axis_size("seq") * stream.shape[0],), dtype=jnp.bool_)
    normed_cross, cross_pullback = jax.vjp(modulated_norm, stream, shifts[0], shifts[1])
    normed_cross = normed_cross.astype(jnp.bfloat16)
    query_cross = product(normed_cross, q_full).astype(jnp.bfloat16)
    image_kv = product(image_rows, kv_full)
    image_keys = image_kv[:, :width].astype(jnp.bfloat16)
    image_values = image_kv[:, width:].astype(jnp.bfloat16)
    attended_cross, cross_stats = attend_forward(query_cross, image_keys, image_values, valid)
    attended_cross = attended_cross.astype(jnp.bfloat16)
    after_cross = stream + product(attended_cross, out_cross_full)
    normed_self, self_pullback = jax.vjp(modulated_norm, after_cross, shifts[2], shifts[3])
    normed_self = normed_self.astype(jnp.bfloat16)
    packed = product(normed_self, qkv_full).astype(jnp.bfloat16)
    query_self = packed[:, :width]
    key_local = packed[:, width : 2 * width]
    value_local = packed[:, 2 * width :]
    key_whole, value_whole = (
        lax.all_gather(key_local, "seq", axis=0, tiled=True),
        lax.all_gather(value_local, "seq", axis=0, tiled=True),
    )
    attended_self, self_stats = attend_forward(query_self, key_whole, value_whole, everywhere)
    attended_self = attended_self.astype(jnp.bfloat16)
    after_self = after_cross + product(attended_self, out_self_full)
    normed_mlp, mlp_pullback = jax.vjp(modulated_norm, after_self, shifts[4], shifts[5])
    normed_mlp = normed_mlp.astype(jnp.bfloat16)
    up_rows = product(normed_mlp, mlp_in_full)
    hidden, gelu_pullback = jax.vjp(jax.nn.gelu, up_rows)
    hidden = hidden.astype(jnp.bfloat16)
    output = after_self + product(hidden, mlp_out_full)
    grad_stream = cotangent[0].astype(jnp.float32)
    grad_branch = grad_stream.astype(jnp.bfloat16)
    grad_mlp_out = contract_rows(hidden, grad_branch)
    (grad_up,) = gelu_pullback(times_transposed(grad_branch, mlp_out_full))
    grad_up = grad_up.astype(jnp.bfloat16)
    grad_mlp_in = contract_rows(normed_mlp, grad_up)
    grad_from, shift_mlp, scale_mlp = mlp_pullback(times_transposed(grad_up, mlp_in_full))
    grad_stream = grad_stream + grad_from
    grad_branch = grad_stream.astype(jnp.bfloat16)
    grad_out_self = contract_rows(attended_self, grad_branch)
    grad_attended = times_transposed(grad_branch, out_self_full).astype(jnp.bfloat16)
    grad_query, inner_local, key_terms, value_terms = attend_backward(
        query_self, key_whole, value_whole, everywhere, self_stats, grad_attended
    )
    grad_key, grad_value = (
        lax.psum_scatter(key_terms, "seq", scatter_dimension=0, tiled=True),
        lax.psum_scatter(value_terms, "seq", scatter_dimension=0, tiled=True),
    )
    grad_packed = jnp.concatenate([grad_query, grad_key, grad_value], axis=1).astype(jnp.bfloat16)
    grad_qkv_self = contract_rows(normed_self, grad_packed)
    grad_from, shift_self, scale_self = self_pullback(times_transposed(grad_packed, qkv_full))
    grad_stream = grad_stream + grad_from
    grad_branch = grad_stream.astype(jnp.bfloat16)
    grad_out_cross = contract_rows(attended_cross, grad_branch)
    grad_attended = times_transposed(grad_branch, out_cross_full).astype(jnp.bfloat16)
    grad_query, inner_cross, key_terms, value_terms = attend_backward(
        query_cross, image_keys, image_values, valid, cross_stats, grad_attended
    )
    image_float = image_rows.astype(jnp.float32)
    image_key_grad, image_value_grad = (
        lax.psum_scatter(
            key_terms.astype(jnp.bfloat16), "seq", scatter_dimension=1, tiled=True
        ).astype(jnp.float32),
        lax.psum_scatter(
            value_terms.astype(jnp.bfloat16), "seq", scatter_dimension=1, tiled=True
        ).astype(jnp.float32),
    )
    block_width = image_key_grad.shape[1]
    column_start = lax.axis_index("seq") * block_width
    image_grads = jnp.concatenate([image_key_grad, image_value_grad], axis=1)
    kv_block = lax.dot_general(
        image_float,
        image_grads,
        (((0,), (0,)), ((), ())),
        precision=highest,
        preferred_element_type=jnp.float32,
    )
    grad_kv_image = jnp.zeros((image_rows.shape[1], 2 * width), jnp.float32)
    grad_kv_image = lax.dynamic_update_slice(
        grad_kv_image, kv_block[:, :block_width], (jnp.int32(0), column_start)
    )
    grad_kv_image = lax.dynamic_update_slice(
        grad_kv_image, kv_block[:, block_width:], (jnp.int32(0), column_start + width)
    )
    grad_query = grad_query.astype(jnp.bfloat16)
    grad_q_cross = contract_rows(normed_cross, grad_query)
    grad_from, shift_cross, scale_cross = cross_pullback(times_transposed(grad_query, q_full))
    grad_input = grad_stream + grad_from
    grad_row = jnp.concatenate(
        [shift_cross, scale_cross, shift_self, scale_self, shift_mlp, scale_mlp]
    )
    grad_table = lax.dynamic_update_slice(
        jnp.zeros(modulation_all.shape, jnp.float32),
        grad_row[None, :],
        (object_index, jnp.int32(0)),
    )
    grad_table = lax.psum(grad_table, ("batch", "seq"))
    grad_modulation = lax.dot_general(
        camera_gate.astype(jnp.float32),
        grad_table,
        (((0,), (0,)), ((), ())),
        precision=highest,
        preferred_element_type=jnp.float32,
    )
    terms = (
        grad_q_cross,
        grad_kv_image,
        grad_out_cross,
        grad_qkv_self,
        grad_out_self,
        grad_mlp_in,
        grad_mlp_out,
    )
    shares = (
        lax.psum_scatter(
            terms[0].astype(jnp.bfloat16), "batch", scatter_dimension=0, tiled=True
        ).astype(jnp.float32),
        lax.psum_scatter(
            terms[1].astype(jnp.bfloat16), "batch", scatter_dimension=0, tiled=True
        ).astype(jnp.float32),
        lax.psum_scatter(
            terms[2].astype(jnp.bfloat16), "batch", scatter_dimension=0, tiled=True
        ).astype(jnp.float32),
        lax.psum_scatter(
            terms[3].astype(jnp.bfloat16), "batch", scatter_dimension=0, tiled=True
        ).astype(jnp.float32),
        lax.psum_scatter(
            terms[4].astype(jnp.bfloat16), "batch", scatter_dimension=0, tiled=True
        ).astype(jnp.float32),
        lax.psum_scatter(
            terms[5].astype(jnp.bfloat16), "batch", scatter_dimension=0, tiled=True
        ).astype(jnp.float32),
        lax.psum_scatter(
            terms[6].astype(jnp.bfloat16), "batch", scatter_dimension=0, tiled=True
        ).astype(jnp.float32),
    )
    totals = (
        lax.psum(shares[0].astype(jnp.bfloat16), "seq").astype(jnp.float32),
        lax.psum(shares[1].astype(jnp.bfloat16), "seq").astype(jnp.float32),
        lax.psum(shares[2].astype(jnp.bfloat16), "seq").astype(jnp.float32),
        lax.psum(shares[3].astype(jnp.bfloat16), "seq").astype(jnp.float32),
        lax.psum(shares[4].astype(jnp.bfloat16), "seq").astype(jnp.float32),
        lax.psum(shares[5].astype(jnp.bfloat16), "seq").astype(jnp.float32),
        lax.psum(shares[6].astype(jnp.bfloat16), "seq").astype(jnp.float32),
    )
    return (
        output.astype(jnp.bfloat16)[None],
        grad_input[None],
        grad_modulation,
        totals[0],
        totals[1],
        totals[2],
        totals[3],
        totals[4],
        totals[5],
        totals[6],
    )


def solution(mesh):
    return jax.shard_map(
        local,
        mesh=mesh,
        in_specs=(
            P("batch", "seq", None),
            P("batch", "seq", None),
            P("batch", None, None),
            P("batch"),
            P("batch", None),
            P(None, "batch"),
            P("batch", None),
            P("batch", None),
            P("batch", None),
            P("batch", None),
            P("batch", None),
            P("batch", None),
            P("batch", None),
            P("batch", None),
        ),
        out_specs=(
            P("batch", "seq", None),
            P("batch", "seq", None),
            P("batch", None),
            P("batch", None),
            P("batch", None),
            P("batch", None),
            P("batch", None),
            P("batch", None),
            P("batch", None),
            P("batch", None),
        ),
        check_vma=False,
    )
```

profile of v0, /device:TPU:0, one launch (start us, length us, event | category | flops | bytes accessed | tf_op | source)
XLA Modules:
  0.0 1926.2 jit_solution(18248695921334428257)
XLA Ops:
  15.5 69.2 %all-reduce.5.cloned.1.call-done = f32[8,6144]{1,0:T(8,128)} async-done(((f32[8,6144]{1,0:T(8,128)}), f32[8,6144]{1,0:T(8,128)}) %all-reduce.5.cloned.1.call-update) | async-done | bytes 196624 | tf_op jit(solution)/shard_map/psum | solution.py:140
  85.7 49.7 %all-gather.10.cloned.1.call-done = bf16[1024,1024]{1,0:T(8,128)(2,1)} async-done(((bf16[128,1024]{1,0:T(8,128)(2,1)}), bf16[1024,1024]{1,0:T(8,128)(2,1)}) %all-gather.10.cloned.1.call-update) | async-done | bytes 2097168 | tf_op jit(solution)/shard_map/all_gather | solution.py:131
  138.0 58.8 %all-gather.12.cloned.1.call-done = bf16[768,2048]{1,0:T(8,128)(2,1)} async-done(((bf16[96,2048]{1,0:T(8,128)(2,1)}), bf16[768,2048]{1,0:T(8,128)(2,1)}) %all-gather.12.cloned.1.call-update) | async-done | bytes 3145744 | tf_op jit(solution)/shard_map/all_gather | solution.py:132
  213.2 18.4 while.56
  249.9 96.9 %all-gather.16.cloned.1.call-done = bf16[1024,3072]{1,0:T(8,128)(2,1)} async-done(((bf16[128,3072]{1,0:T(8,128)(2,1)}), bf16[1024,3072]{1,0:T(8,128)(2,1)}) %all-gather.16.cloned.1.call-update) | async-done | bytes 6291472 | tf_op jit(solution)/shard_map/all_gather | solution.py:134
  377.6 20.9 %all-gather.20.cloned.1.call-done = bf16[1024,1024]{1,0:T(8,128)(2,1)} async-done(((bf16[256,1024]{1,0:T(8,128)(2,1)}), bf16[1024,1024]{1,0:T(8,128)(2,1)}) %all-gather.20.cloned.1.call-update) | async-done | bytes 2097168 | tf_op jit(solution)/shard_map/all_gather | solution.py:168
  403.3 23.0 %while.57 = (s32[]{:T(128)}, bf16[4,4,256,64]{2,3,1,0:T(8,128)(2,1)}, f32[4,4,256,1]{2,1,3,0:T(4,128)S(1)}, f32[4,4,256,1]{2,1,3,0:T(4,128)S(1)}, bf16[4,4,256,6...) while((s32[]{:T(128)}, ...), condition=%wide.region_12.13_spmd, body=%wide.region_9.12_spmd.sunk | while | flops 277870592 | bytes 18258072 | solution.py:65
  426.2 24.1 %all-gather.22.cloned.1.call-done = bf16[1024,1024]{1,0:T(8,128)(2,1)} async-done(((bf16[128,1024]{1,0:T(8,128)(2,1)}), bf16[1024,1024]{1,0:T(8,128)(2,1)}) %all-gather.22.cloned.1.call-update) | async-done | bytes 2097168 | tf_op jit(solution)/shard_map/all_gather | solution.py:135
  454.2 122.0 %all-gather.24.cloned.1.call-done = bf16[1024,4096]{1,0:T(8,128)(2,1)} async-done(((bf16[128,4096]{1,0:T(8,128)(2,1)}), bf16[1024,4096]{1,0:T(8,128)(2,1)}) %all-gather.24.cloned.1.call-update) | async-done | bytes 8388624 | tf_op jit(solution)/shard_map/all_gather | solution.py:136
  584.3 117.2 %all-gather.26.cloned.1.call-done = bf16[4096,1024]{1,0:T(8,128)(2,1)} async-done(((bf16[512,1024]{1,0:T(8,128)(2,1)}), bf16[4096,1024]{1,0:T(8,128)(2,1)}) %all-gather.26.cloned.1.call-update) | async-done | bytes 8388624 | tf_op jit(solution)/shard_map/all_gather | solution.py:137
  720.9 39.8 %while.58 = (s32[]{:T(128)}, bf16[4,4,256,64]{2,3,1,0:T(8,128)(2,1)}, f32[4,4,1024,64]{2,3,1,0:T(8,128)}, f32[4,4,1024,64]{2,3,1,0:T(8,128)}, bf16[4,4,256,64]{2...) while((s32[]{:T(128)}, ...), condition=%wide.region_19.20_spmd, body=%wide.region_17.19_spmd.sunk | while | flops 680852480 | bytes 48534732 | solution.py:100
  761.4 42.2 %reduce-scatter.14.cloned.1.call-done = f32[256,1024]{0,1:T(8,128)} async-done(((f32[1024,1024]{0,1:T(8,128)}), f32[256,1024]{0,1:T(8,128)}) %reduce-scatter.14.cloned.1.call-update) | async-done | bytes 1048592 | tf_op jit(solution)/shard_map/reduce_scatter | solution.py:195
  804.9 45.6 %reduce-scatter.12.cloned.1.call-done = f32[256,1024]{0,1:T(8,128)} async-done(((f32[1024,1024]{0,1:T(8,128)}), f32[256,1024]{0,1:T(8,128)}) %reduce-scatter.12.cloned.1.call-update) | async-done | bytes 1048592 | tf_op jit(solution)/shard_map/reduce_scatter | solution.py:194
  863.9 40.3 %while.59 = (s32[]{:T(128)}, bf16[4,4,256,64]{2,3,1,0:T(8,128)(2,1)}, bf16[4,4,1025,64]{2,3,1,0:T(8,128)(2,1)}, bf16[4,4,1025,64]{2,3,1,0:T(8,128)(2,1)}, pred[1...) while((s32[]{:T(128)}, ...), condition=%wide.region_26.27_spmd, body=%wide.region_24.26_spmd.sunk | while | flops 682566912 | bytes 82707776 | solution.py:100
  937.4 35.5 %reduce-scatter.18.cloned.1.call-done = bf16[1025,256]{0,1:T(8,128)(2,1)} async-done(((bf16[1025,1024]{0,1:T(8,128)(2,1)}), bf16[1025,256]{0,1:T(8,128)(2,1)}) %reduce-scatter.18.cloned.1.call-update) | async-done | bytes 524816 | tf_op jit(solution)/shard_map/reduce_scatter | solution.py:209
  995.6 48.8 %reduce-scatter.28.cloned.1.call-done = bf16[128,1024]{1,0:T(8,128)(2,1)} async-done(((bf16[1024,1024]{1,0:T(8,128)(2,1)}), bf16[128,1024]{1,0:T(8,128)(2,1)}) %reduce-scatter.28.cloned.1.call-update) | async-done | bytes 262160 | tf_op jit(solution)/shard_map/reduce_scatter | solution.py:275
  1044.4 71.2 %reduce-scatter.16.cloned.1.call-done = bf16[128,1024]{1,0:T(8,128)(2,1)} async-done(((bf16[1024,1024]{1,0:T(8,128)(2,1)}), bf16[128,1024]{1,0:T(8,128)(2,1)}) %reduce-scatter.16.cloned.1.call-update) | async-done | bytes 262160 | tf_op jit(solution)/shard_map/reduce_scatter | solution.py:263
  1115.6 71.3 %reduce-scatter.24.cloned.1.call-done = bf16[128,1024]{1,0:T(8,128)(2,1)} async-done(((bf16[1024,1024]{1,0:T(8,128)(2,1)}), bf16[128,1024]{1,0:T(8,128)(2,1)}) %reduce-scatter.24.cloned.1.call-update) | async-done | bytes 262160 | tf_op jit(solution)/shard_map/reduce_scatter | solution.py:269
  1186.9 152.0 %reduce-scatter.30.cloned.1.call-done = bf16[128,4096]{1,0:T(8,128)(2,1)} async-done(((bf16[1024,4096]{1,0:T(8,128)(2,1)}), bf16[128,4096]{1,0:T(8,128)(2,1)}) %reduce-scatter.30.cloned.1.call-update) | async-done | bytes 1048592 | tf_op jit(solution)/shard_map/reduce_scatter | solution.py:278
  1338.9 151.7 %reduce-scatter.32.cloned.1.call-done = bf16[512,1024]{1,0:T(8,128)(2,1)} async-done(((bf16[4096,1024]{1,0:T(8,128)(2,1)}), bf16[512,1024]{1,0:T(8,128)(2,1)}) %reduce-scatter.32.cloned.1.call-update) | async-done | bytes 1048592 | tf_op jit(solution)/shard_map/reduce_scatter | solution.py:281
  1490.6 77.8 %reduce-scatter.22.cloned.1.call-done = bf16[96,2048]{1,0:T(8,128)(2,1)} async-done(((bf16[768,2048]{1,0:T(8,128)(2,1)}), bf16[96,2048]{1,0:T(8,128)(2,1)}) %reduce-scatter.22.cloned.1.call-update) | async-done | bytes 393232 | tf_op jit(solution)/shard_map/reduce_scatter | solution.py:266
  1568.4 121.2 %reduce-scatter.26.cloned.1.call-done = bf16[128,3072]{1,0:T(8,128)(2,1)} async-done(((bf16[1024,3072]{1,0:T(8,128)(2,1)}), bf16[128,3072]{1,0:T(8,128)(2,1)}) %reduce-scatter.26.cloned.1.call-update) | async-done | bytes 786448 | tf_op jit(solution)/shard_map/reduce_scatter | solution.py:272
  1699.4 119.4 %all-reduce.7.cloned.1.call-done = f32[8,6144]{1,0:T(8,128)} async-done(((f32[8,6144]{1,0:T(8,128)}), f32[8,6144]{1,0:T(8,128)}) %all-reduce.7.cloned.1.call-update) | async-done | bytes 196624 | tf_op jit(solution)/shard_map/psum | solution.py:245
  1822.9 84.5 %all-reduce.9.cloned.1.call-done = (bf16[128,1024]{1,0:T(8,128)(2,1)}, bf16[96,2048]{1,0:T(8,128)(2,1)}, bf16[128,1024]{1,0:T(8,128)(2,1)}, bf16[128,3072]{1,0:T...) async-done(((bf16[128,1024]{1,0:T(8,128)(2,1)}, bf16[96,2048]{1,0:T(8,128)(2,1)}, bf16[128,1024]{1,0:T(8,128)(2,1)}, ...) | async-done | bytes 4063248 | tf_op jit(solution)/shard_map/psum | solution.py:286
  (443 shorter events, 328.9 us)
Async XLA Ops:
  7.2 77.5 %all-reduce.5.cloned.1.call-start = ((), (), s32[]{:S(2)}) async-start(), calls=%async_computation.11 | async-start | bytes 393216 | tf_op jit(solution)/shard_map/psum | solution.py:140
  9.8 125.6 %all-gather.10.cloned.1.call-start = ((), (), s32[]{:S(2)}) async-start(), calls=%async_computation.12 | async-start | bytes 2359296 | tf_op jit(solution)/shard_map/all_gather | solution.py:131
  10.6 186.2 %all-gather.12.cloned.1.call-start = ((), (), s32[]{:S(2)}) async-start(), calls=%async_computation.13 | async-start | bytes 3538944 | tf_op jit(solution)/shard_map/all_gather | solution.py:132
  11.3 235.6 %all-gather.14.cloned.1.call-start = ((), (), s32[]{:S(2)}) async-start(), calls=%async_computation.14 | async-start | bytes 2359296 | tf_op jit(solution)/shard_map/all_gather | solution.py:133
  11.9 334.9 %all-gather.16.cloned.1.call-start = ((), (), s32[]{:S(2)}) async-start(), calls=%async_computation.15 | async-start | bytes 7077888 | tf_op jit(solution)/shard_map/all_gather | solution.py:134
  12.5 361.1 %all-gather.18.cloned.1.call-start = ((), (), s32[]{:S(2)}) async-start(), calls=%async_computation.16 | async-start | bytes 2621440 | tf_op jit(solution)/shard_map/all_gather | solution.py:167
  352.7 45.8 %all-gather.20.cloned.1.call-start = ((), (), s32[]{:S(2)}) async-start(), calls=%async_computation.17 | async-start | bytes 2621440 | tf_op jit(solution)/shard_map/all_gather | solution.py:168
  353.4 96.9 %all-gather.22.cloned.1.call-start = ((), (), s32[]{:S(2)}) async-start(), calls=%async_computation.18 | async-start | bytes 2359296 | tf_op jit(solution)/shard_map/all_gather | solution.py:135
  354.2 222.0 %all-gather.24.cloned.1.call-start = ((), (), s32[]{:S(2)}) async-start(), calls=%async_computation.19 | async-start | bytes 9437184 | tf_op jit(solution)/shard_map/all_gather | solution.py:136
  354.9 346.6 %all-gather.26.cloned.1.call-start = ((), (), s32[]{:S(2)}) async-start(), calls=%async_computation.20 | async-start | bytes 9437184 | tf_op jit(solution)/shard_map/all_gather | solution.py:137
  355.5 448.1 %reduce-scatter.14.cloned.1.call-start = ((), (), s32[]{:S(2)}) async-start(), calls=%async_computation.22 | async-start | bytes 5242880 | tf_op jit(solution)/shard_map/reduce_scatter | solution.py:195
  760.8 89.7 %reduce-scatter.12.cloned.1.call-start = ((), (), s32[]{:S(2)}) async-start(), calls=%async_computation.21 | async-start | bytes 5242880 | tf_op jit(solution)/shard_map/reduce_scatter | solution.py:194
  761.3 176.1 %reduce-scatter.20.cloned.1.call-start = ((), (), s32[]{:S(2)}) async-start(), calls=%async_computation.26 | async-start | bytes 2949120 | tf_op jit(solution)/shard_map/reduce_scatter | solution.py:212
  904.3 68.7 %reduce-scatter.18.cloned.1.call-start = ((), (), s32[]{:S(2)}) async-start(), calls=%async_computation.25 | async-start | bytes 2949120 | tf_op jit(solution)/shard_map/reduce_scatter | solution.py:209
  904.9 139.5 %reduce-scatter.28.cloned.1.call-start = ((), (), s32[]{:S(2)}) async-start(), calls=%async_computation.30 | async-start | bytes 2359296 | tf_op jit(solution)/shard_map/reduce_scatter | solution.py:275
  908.2 207.4 %reduce-scatter.16.cloned.1.call-start = ((), (), s32[]{:S(2)}) async-start(), calls=%async_computation.24 | async-start | bytes 2359296 | tf_op jit(solution)/shard_map/reduce_scatter | solution.py:263
  911.8 275.1 %reduce-scatter.24.cloned.1.call-start = ((), (), s32[]{:S(2)}) async-start(), calls=%async_computation.28 | async-start | bytes 2359296 | tf_op jit(solution)/shard_map/reduce_scatter | solution.py:269
  915.5 423.4 %reduce-scatter.30.cloned.1.call-start = ((), (), s32[]{:S(2)}) async-start(), calls=%async_computation.31 | async-start | bytes 9437184 | tf_op jit(solution)/shard_map/reduce_scatter | solution.py:278
  923.3 567.3 %reduce-scatter.32.cloned.1.call-start = ((), (), s32[]{:S(2)}) async-start(), calls=%async_computation.32 | async-start | bytes 9437184 | tf_op jit(solution)/shard_map/reduce_scatter | solution.py:281
  932.0 636.4 %reduce-scatter.22.cloned.1.call-start = ((), (), s32[]{:S(2)}) async-start(), calls=%async_computation.27 | async-start | bytes 3538944 | tf_op jit(solution)/shard_map/reduce_scatter | solution.py:266
  982.9 706.8 %reduce-scatter.26.cloned.1.call-start = ((), (), s32[]{:S(2)}) async-start(), calls=%async_computation.29 | async-start | bytes 7077888 | tf_op jit(solution)/shard_map/reduce_scatter | solution.py:272
  989.3 700.4 %copy-start.5 = (f32[256,1024]{1,0:T(8,128)S(1)}, f32[256,1024]{1,0:T(8,128)}, u32[]{:S(2)}) copy-start(f32[256,1024]{1,0:T(8,128)} %copy-done.3) | copy-start | bytes 3145732
  989.3 829.5 %all-reduce.7.cloned.1.call-start = ((), (), s32[]{:S(2)}) async-start(), calls=%async_computation.23 | async-start | bytes 393216 | tf_op jit(solution)/shard_map/psum | solution.py:245
  995.5 911.8 %all-reduce.9.cloned.1.call-start = ((), (), s32[]{:S(2)}) async-start(), calls=%async_computation.33 | async-start | bytes 8126464 | tf_op jit(solution)/shard_map/psum | solution.py:286
  (106 other events, 4647.0 us)
Sparse Core Ops, SparseCore 0:
  11.9 72.7 all-reduce.4
  87.1 48.3 all-gather.9
  137.9 58.9 all-gather.11
  199.0 47.9 all-gather.13
  249.2 97.5 all-gather.15
  352.8 20.7 all-gather.17
  375.8 22.5 all-gather.19
  400.8 49.5 all-gather.21
  452.7 123.4 all-gather.23
  578.4 123.1 all-gather.25
  760.9 42.6 reduce-scatter.13
  806.0 44.4 reduce-scatter.11
  904.3 33.0 reduce-scatter.19
  939.8 33.0 reduce-scatter.17
  976.7 67.6 reduce-scatter.27
  1048.8 66.7 reduce-scatter.15
  1120.0 66.8 reduce-scatter.23
  1190.8 148.0 reduce-scatter.29
  1342.5 147.9 reduce-scatter.31
  1495.0 73.3 reduce-scatter.21
  1572.4 117.1 reduce-scatter.25
  1696.7 122.1 all-reduce.6
  1822.0 85.3 all-reduce.8
where the time goes:
time: 1940 us; the launch traced here: 1930 us
  waiting for transfers between devices  1620 us (84%)
  matrix products  195 us (10%)
  local copies, waits for them, and re-layouts  57.6 us (3%)
  other arithmetic  31.7 us (2%)
    reduce_scatter x1, waiting for transfers between devices, local(): lax.psum_scatter(terms[5].astype(jnp.bfloat16), 'batch', scatter_dimensio...  152 us
    reduce_scatter x1, waiting for transfers between devices, local(): lax.psum_scatter(terms[6].astype(jnp.bfloat16), 'batch', scatter_dimensio...  152 us
    all_gather x1, waiting for transfers between devices, local(): lax.all_gather(mlp_in, 'batch', axis=0, tiled=True)  122 us
    reduce_scatter x1, waiting for transfers between devices, local(): lax.psum_scatter(terms[3].astype(jnp.bfloat16), 'batch', scatter_dimensio...  121 us
    psum x1, waiting for transfers between devices, local(): grad_table = lax.psum(grad_table, ('batch', 'seq'))  119 us
    all_gather x1, waiting for transfers between devices, local(): lax.all_gather(mlp_out, 'batch', axis=0, tiled=True)  117 us
    all_gather x1, waiting for transfers between devices, local(): lax.all_gather(qkv_self, 'batch', axis=0, tiled=True)  96.9 us
    psum x1, waiting for transfers between devices, local(): lax.psum(shares[0].astype(jnp.bfloat16), 'seq').astype(jnp.float32)  84.5 us
  transfers between devices with their start and end apart: 23, of which 23 were waited for; matrix products, arithmetic and copies ran while one was open for 8% of the time, Pallas kernels for 0%

commit v1 on v0

--- a/solution.py
+++ b/solution.py
@@ -283,7 +283,7 @@
         ).astype(jnp.float32),
     )
     totals = (
-        lax.psum(shares[0].astype(jnp.bfloat16), "seq").astype(jnp.float32),
+        jnp.sum(lax.all_gather(shares[0].astype(jnp.bfloat16), "seq"), axis=0).astype(jnp.float32),
         lax.psum(shares[1].astype(jnp.bfloat16), "seq").astype(jnp.float32),
         lax.psum(shares[2].astype(jnp.bfloat16), "seq").astype(jnp.float32),
         lax.psum(shares[3].astype(jnp.bfloat16), "seq").astype(jnp.float32),

time: 1940 us -> 1950 us (level)
    reduce_scatter x1, waiting for transfers between devices: 48.8 us -> 70.6 us  [local(): lax.psum_scatter(terms[4].astype(jnp.bfloat16), 'batch', scatter_dimensio...]
    reduce_scatter x1, waiting for transfers between devices: 71.2 us -> 49.5 us  [local(): lax.psum_scatter(terms[0].astype(jnp.bfloat16), 'batch', scatter_dimensio...]
  transfers between devices with their start and end apart: 23 -> 24, of which waited for: 23 -> 24; matrix products, arithmetic and copies ran while one was open for 8% -> 8% of each run, Pallas kernels for 0% -> 0%
where the time goes in v1:
time: 1950 us; the launch traced here: 1940 us
  waiting for transfers between devices  1630 us (84%)
  matrix products  195 us (10%)
  local copies, waits for them, and re-layouts  57.9 us (3%)
  other arithmetic  32.1 us (2%)
    reduce_scatter x1, waiting for transfers between devices, local(): lax.psum_scatter(terms[5].astype(jnp.bfloat16), 'batch', scatter_dimensio...  152 us
    reduce_scatter x1, waiting for transfers between devices, local(): lax.psum_scatter(terms[6].astype(jnp.bfloat16), 'batch', scatter_dimensio...  152 us
    all_gather x1, waiting for transfers between devices, local(): lax.all_gather(mlp_in, 'batch', axis=0, tiled=True)  122 us
    reduce_scatter x1, waiting for transfers between devices, local(): lax.psum_scatter(terms[3].astype(jnp.bfloat16), 'batch', scatter_dimensio...  121 us
    psum x1, waiting for transfers between devices, local(): grad_table = lax.psum(grad_table, ('batch', 'seq'))  119 us
    all_gather x1, waiting for transfers between devices, local(): lax.all_gather(mlp_out, 'batch', axis=0, tiled=True)  117 us
    all_gather x1, waiting for transfers between devices, local(): lax.all_gather(qkv_self, 'batch', axis=0, tiled=True)  96.9 us
    psum x1, waiting for transfers between devices, local(): lax.psum(shares[1].astype(jnp.bfloat16), 'seq').astype(jnp.float32)  80.6 us
  transfers between devices with their start and end apart: 24, of which 24 were waited for; matrix products, arithmetic and copies ran while one was open for 8% of the time, Pallas kernels for 0%

profile of v1, /device:TPU:0, one launch (start us, length us, event | category | flops | bytes accessed | tf_op | source)
XLA Modules:
  0.0 1938.4 jit_solution(13779485756038650673)
XLA Ops:
  15.5 69.2 %all-reduce.5.cloned.1.call-done = f32[8,6144]{1,0:T(8,128)} async-done(((f32[8,6144]{1,0:T(8,128)}), f32[8,6144]{1,0:T(8,128)}) %all-reduce.5.cloned.1.call-update) | async-done | bytes 196624 | tf_op jit(solution)/shard_map/psum | solution.py:140
  85.7 49.7 %all-gather.12.cloned.1.call-done = bf16[1024,1024]{1,0:T(8,128)(2,1)} async-done(((bf16[128,1024]{1,0:T(8,128)(2,1)}), bf16[1024,1024]{1,0:T(8,128)(2,1)}) %all-gather.12.cloned.1.call-update) | async-done | bytes 2097168 | tf_op jit(solution)/shard_map/all_gather | solution.py:131
  138.0 58.8 %all-gather.14.cloned.1.call-done = bf16[768,2048]{1,0:T(8,128)(2,1)} async-done(((bf16[96,2048]{1,0:T(8,128)(2,1)}), bf16[768,2048]{1,0:T(8,128)(2,1)}) %all-gather.14.cloned.1.call-update) | async-done | bytes 3145744 | tf_op jit(solution)/shard_map/all_gather | solution.py:132
  213.2 18.4 while.56
  249.9 96.9 %all-gather.18.cloned.1.call-done = bf16[1024,3072]{1,0:T(8,128)(2,1)} async-done(((bf16[128,3072]{1,0:T(8,128)(2,1)}), bf16[1024,3072]{1,0:T(8,128)(2,1)}) %all-gather.18.cloned.1.call-update) | async-done | bytes 6291472 | tf_op jit(solution)/shard_map/all_gather | solution.py:134
  377.6 20.9 %all-gather.22.cloned.1.call-done = bf16[1024,1024]{1,0:T(8,128)(2,1)} async-done(((bf16[256,1024]{1,0:T(8,128)(2,1)}), bf16[1024,1024]{1,0:T(8,128)(2,1)}) %all-gather.22.cloned.1.call-update) | async-done | bytes 2097168 | tf_op jit(solution)/shard_map/all_gather | solution.py:168
  403.3 23.0 %while.57 = (s32[]{:T(128)}, bf16[4,4,256,64]{2,3,1,0:T(8,128)(2,1)}, f32[4,4,256,1]{2,1,3,0:T(4,128)S(1)}, f32[4,4,256,1]{2,1,3,0:T(4,128)S(1)}, bf16[4,4,256,6...) while((s32[]{:T(128)}, ...), condition=%wide.region_12.13_spmd, body=%wide.region_9.12_spmd.sunk | while | flops 277870592 | bytes 18258072 | solution.py:65
  426.2 24.1 %all-gather.24.cloned.1.call-done = bf16[1024,1024]{1,0:T(8,128)(2,1)} async-done(((bf16[128,1024]{1,0:T(8,128)(2,1)}), bf16[1024,1024]{1,0:T(8,128)(2,1)}) %all-gather.24.cloned.1.call-update) | async-done | bytes 2097168 | tf_op jit(solution)/shard_map/all_gather | solution.py:135
  454.2 122.0 %all-gather.26.cloned.1.call-done = bf16[1024,4096]{1,0:T(8,128)(2,1)} async-done(((bf16[128,4096]{1,0:T(8,128)(2,1)}), bf16[1024,4096]{1,0:T(8,128)(2,1)}) %all-gather.26.cloned.1.call-update) | async-done | bytes 8388624 | tf_op jit(solution)/shard_map/all_gather | solution.py:136
  584.3 117.2 %all-gather.28.cloned.1.call-done = bf16[4096,1024]{1,0:T(8,128)(2,1)} async-done(((bf16[512,1024]{1,0:T(8,128)(2,1)}), bf16[4096,1024]{1,0:T(8,128)(2,1)}) %all-gather.28.cloned.1.call-update) | async-done | bytes 8388624 | tf_op jit(solution)/shard_map/all_gather | solution.py:137
  720.9 39.8 %while.58 = (s32[]{:T(128)}, bf16[4,4,256,64]{2,3,1,0:T(8,128)(2,1)}, f32[4,4,1024,64]{2,3,1,0:T(8,128)}, f32[4,4,1024,64]{2,3,1,0:T(8,128)}, bf16[4,4,256,64]{2...) while((s32[]{:T(128)}, ...), condition=%wide.region_19.20_spmd, body=%wide.region_17.19_spmd.sunk | while | flops 680852480 | bytes 48534732 | solution.py:100
  761.4 42.2 %reduce-scatter.14.cloned.1.call-done = f32[256,1024]{0,1:T(8,128)} async-done(((f32[1024,1024]{0,1:T(8,128)}), f32[256,1024]{0,1:T(8,128)}) %reduce-scatter.14.cloned.1.call-update) | async-done | bytes 1048592 | tf_op jit(solution)/shard_map/reduce_scatter | solution.py:195
  804.9 45.6 %reduce-scatter.12.cloned.1.call-done = f32[256,1024]{0,1:T(8,128)} async-done(((f32[1024,1024]{0,1:T(8,128)}), f32[256,1024]{0,1:T(8,128)}) %reduce-scatter.12.cloned.1.call-update) | async-done | bytes 1048592 | tf_op jit(solution)/shard_map/reduce_scatter | solution.py:194
  863.9 40.3 %while.59 = (s32[]{:T(128)}, bf16[4,4,256,64]{2,3,1,0:T(8,128)(2,1)}, bf16[4,4,1025,64]{2,3,1,0:T(8,128)(2,1)}, bf16[4,4,1025,64]{2,3,1,0:T(8,128)(2,1)}, pred[1...) while((s32[]{:T(128)}, ...), condition=%wide.region_26.27_spmd, body=%wide.region_24.26_spmd.sunk | while | flops 682566912 | bytes 82707776 | solution.py:100
  937.4 35.5 %reduce-scatter.18.cloned.1.call-done = bf16[1025,256]{0,1:T(8,128)(2,1)} async-done(((bf16[1025,1024]{0,1:T(8,128)(2,1)}), bf16[1025,256]{0,1:T(8,128)(2,1)}) %reduce-scatter.18.cloned.1.call-update) | async-done | bytes 524816 | tf_op jit(solution)/shard_map/reduce_scatter | solution.py:209
  995.5 49.5 %reduce-scatter.16.cloned.1.call-done = bf16[128,1024]{1,0:T(8,128)(2,1)} async-done(((bf16[1024,1024]{1,0:T(8,128)(2,1)}), bf16[128,1024]{1,0:T(8,128)(2,1)}) %reduce-scatter.16.cloned.1.call-update) | async-done | bytes 262160 | tf_op jit(solution)/shard_map/reduce_scatter | solution.py:263
  1045.0 70.6 %reduce-scatter.28.cloned.1.call-done = bf16[128,1024]{1,0:T(8,128)(2,1)} async-done(((bf16[1024,1024]{1,0:T(8,128)(2,1)}), bf16[128,1024]{1,0:T(8,128)(2,1)}) %reduce-scatter.28.cloned.1.call-update) | async-done | bytes 262160 | tf_op jit(solution)/shard_map/reduce_scatter | solution.py:275
  1115.6 71.3 %reduce-scatter.24.cloned.1.call-done = bf16[128,1024]{1,0:T(8,128)(2,1)} async-done(((bf16[1024,1024]{1,0:T(8,128)(2,1)}), bf16[128,1024]{1,0:T(8,128)(2,1)}) %reduce-scatter.24.cloned.1.call-update) | async-done | bytes 262160 | tf_op jit(solution)/shard_map/reduce_scatter | solution.py:269
  1186.8 152.0 %reduce-scatter.30.cloned.1.call-done = bf16[128,4096]{1,0:T(8,128)(2,1)} async-done(((bf16[1024,4096]{1,0:T(8,128)(2,1)}), bf16[128,4096]{1,0:T(8,128)(2,1)}) %reduce-scatter.30.cloned.1.call-update) | async-done | bytes 1048592 | tf_op jit(solution)/shard_map/reduce_scatter | solution.py:278
  1338.9 151.7 %reduce-scatter.32.cloned.1.call-done = bf16[512,1024]{1,0:T(8,128)(2,1)} async-done(((bf16[4096,1024]{1,0:T(8,128)(2,1)}), bf16[512,1024]{1,0:T(8,128)(2,1)}) %reduce-scatter.32.cloned.1.call-update) | async-done | bytes 1048592 | tf_op jit(solution)/shard_map/reduce_scatter | solution.py:281
  1490.6 77.9 %reduce-scatter.22.cloned.1.call-done = bf16[96,2048]{1,0:T(8,128)(2,1)} async-done(((bf16[768,2048]{1,0:T(8,128)(2,1)}), bf16[96,2048]{1,0:T(8,128)(2,1)}) %reduce-scatter.22.cloned.1.call-update) | async-done | bytes 393232 | tf_op jit(solution)/shard_map/reduce_scatter | solution.py:266
  1568.4 121.2 %reduce-scatter.26.cloned.1.call-done = bf16[128,3072]{1,0:T(8,128)(2,1)} async-done(((bf16[1024,3072]{1,0:T(8,128)(2,1)}), bf16[128,3072]{1,0:T(8,128)(2,1)}) %reduce-scatter.26.cloned.1.call-update) | async-done | bytes 786448 | tf_op jit(solution)/shard_map/reduce_scatter | solution.py:272
  1699.4 119.4 %all-reduce.7.cloned.1.call-done = f32[8,6144]{1,0:T(8,128)} async-done(((f32[8,6144]{1,0:T(8,128)}), f32[8,6144]{1,0:T(8,128)}) %all-reduce.7.cloned.1.call-update) | async-done | bytes 196624 | tf_op jit(solution)/shard_map/psum | solution.py:245
  1840.5 80.6 %all-reduce.9.cloned.1.call-done = (bf16[96,2048]{1,0:T(8,128)(2,1)}, bf16[128,1024]{1,0:T(8,128)(2,1)}, bf16[128,3072]{1,0:T(8,128)(2,1)}, bf16[128,1024]{1,0:T...) async-done(((bf16[96,2048]{1,0:T(8,128)(2,1)}, bf16[128,1024]{1,0:T(8,128)(2,1)}, bf16[128,3072]{1,0:T(8,128)(2,1)}, bf16[128,1024]{1,0:T(8,128)(2,1)}, ...) | async-done | bytes 3801104 | tf_op jit(solution)/shard_map/psum | solution.py:287
  (447 shorter events, 344.6 us)
Async XLA Ops:
  7.2 77.5 %all-reduce.5.cloned.1.call-start = ((), (), s32[]{:S(2)}) async-start(), calls=%async_computation.11 | async-start | bytes 393216 | tf_op jit(solution)/shard_map/psum | solution.py:140
  9.8 125.6 %all-gather.12.cloned.1.call-start = ((), (), s32[]{:S(2)}) async-start(), calls=%async_computation.12 | async-start | bytes 2359296 | tf_op jit(solution)/shard_map/all_gather | solution.py:131
  10.6 186.2 %all-gather.14.cloned.1.call-start = ((), (), s32[]{:S(2)}) async-start(), calls=%async_computation.13 | async-start | bytes 3538944 | tf_op jit(solution)/shard_map/all_gather | solution.py:132
  11.3 235.6 %all-gather.16.cloned.1.call-start = ((), (), s32[]{:S(2)}) async-start(), calls=%async_computation.14 | async-start | bytes 2359296 | tf_op jit(solution)/shard_map/all_gather | solution.py:133
  11.9 334.9 %all-gather.18.cloned.1.call-start = ((), (), s32[]{:S(2)}) async-start(), calls=%async_computation.15 | async-start | bytes 7077888 | tf_op jit(solution)/shard_map/all_gather | solution.py:134
  12.5 361.1 %all-gather.20.cloned.1.call-start = ((), (), s32[]{:S(2)}) async-start(), calls=%async_computation.16 | async-start | bytes 2621440 | tf_op jit(solution)/shard_map/all_gather | solution.py:167
  352.7 45.8 %all-gather.22.cloned.1.call-start = ((), (), s32[]{:S(2)}) async-start(), calls=%async_computation.17 | async-start | bytes 2621440 | tf_op jit(solution)/shard_map/all_gather | solution.py:168
  353.4 96.9 %all-gather.24.cloned.1.call-start = ((), (), s32[]{:S(2)}) async-start(), calls=%async_computation.18 | async-start | bytes 2359296 | tf_op jit(solution)/shard_map/all_gather | solution.py:135
  354.2 222.0 %all-gather.26.cloned.1.call-start = ((), (), s32[]{:S(2)}) async-start(), calls=%async_computation.19 | async-start | bytes 9437184 | tf_op jit(solution)/shard_map/all_gather | solution.py:136
  354.9 346.6 %all-gather.28.cloned.1.call-start = ((), (), s32[]{:S(2)}) async-start(), calls=%async_computation.20 | async-start | bytes 9437184 | tf_op jit(solution)/shard_map/all_gather | solution.py:137
  355.5 448.1 %reduce-scatter.14.cloned.1.call-start = ((), (), s32[]{:S(2)}) async-start(), calls=%async_computation.22 | async-start | bytes 5242880 | tf_op jit(solution)/shard_map/reduce_scatter | solution.py:195
  760.8 89.7 %reduce-scatter.12.cloned.1.call-start = ((), (), s32[]{:S(2)}) async-start(), calls=%async_computation.21 | async-start | bytes 5242880 | tf_op jit(solution)/shard_map/reduce_scatter | solution.py:194
  761.3 176.1 %reduce-scatter.20.cloned.1.call-start = ((), (), s32[]{:S(2)}) async-start(), calls=%async_computation.26 | async-start | bytes 2949120 | tf_op jit(solution)/shard_map/reduce_scatter | solution.py:212
  904.2 68.7 %reduce-scatter.18.cloned.1.call-start = ((), (), s32[]{:S(2)}) async-start(), calls=%async_computation.25 | async-start | bytes 2949120 | tf_op jit(solution)/shard_map/reduce_scatter | solution.py:209
  904.8 140.1 %reduce-scatter.16.cloned.1.call-start = ((), (), s32[]{:S(2)}) async-start(), calls=%async_computation.24 | async-start | bytes 2359296 | tf_op jit(solution)/shard_map/reduce_scatter | solution.py:263
  908.5 207.0 %reduce-scatter.28.cloned.1.call-start = ((), (), s32[]{:S(2)}) async-start(), calls=%async_computation.30 | async-start | bytes 2359296 | tf_op jit(solution)/shard_map/reduce_scatter | solution.py:275
  912.3 274.5 %reduce-scatter.24.cloned.1.call-start = ((), (), s32[]{:S(2)}) async-start(), calls=%async_computation.28 | async-start | bytes 2359296 | tf_op jit(solution)/shard_map/reduce_scatter | solution.py:269
  915.9 423.0 %reduce-scatter.30.cloned.1.call-start = ((), (), s32[]{:S(2)}) async-start(), calls=%async_computation.31 | async-start | bytes 9437184 | tf_op jit(solution)/shard_map/reduce_scatter | solution.py:278
  923.7 566.9 %reduce-scatter.32.cloned.1.call-start = ((), (), s32[]{:S(2)}) async-start(), calls=%async_computation.32 | async-start | bytes 9437184 | tf_op jit(solution)/shard_map/reduce_scatter | solution.py:281
  932.4 636.0 %reduce-scatter.22.cloned.1.call-start = ((), (), s32[]{:S(2)}) async-start(), calls=%async_computation.27 | async-start | bytes 3538944 | tf_op jit(solution)/shard_map/reduce_scatter | solution.py:266
  982.9 706.8 %reduce-scatter.26.cloned.1.call-start = ((), (), s32[]{:S(2)}) async-start(), calls=%async_computation.29 | async-start | bytes 7077888 | tf_op jit(solution)/shard_map/reduce_scatter | solution.py:272
  989.2 829.7 %all-reduce.7.cloned.1.call-start = ((), (), s32[]{:S(2)}) async-start(), calls=%async_computation.23 | async-start | bytes 393216 | tf_op jit(solution)/shard_map/psum | solution.py:245
  995.4 842.8 %all-gather.30.cloned.1.call-start = ((), (), s32[]{:S(2)}) async-start(), calls=%async_computation.33 | async-start | bytes 1310720 | tf_op jit(solution)/shard_map/all_gather | solution.py:286
  1044.9 876.2 %all-reduce.9.cloned.1.call-start = ((), (), s32[]{:S(2)}) async-start(), calls=%async_computation.34 | async-start | bytes 7602176 | tf_op jit(solution)/shard_map/psum | solution.py:287
  (107 other events, 5327.6 us)
Sparse Core Ops, SparseCore 0:
  11.9 72.7 all-reduce.4
  87.1 48.3 all-gather.11
  137.9 58.9 all-gather.13
  199.0 47.9 all-gather.15
  249.2 97.5 all-gather.17
  352.8 20.7 all-gather.19
  375.8 22.5 all-gather.21
  400.8 49.5 all-gather.23
  452.7 123.4 all-gather.25
  578.4 123.1 all-gather.27
  760.9 42.6 reduce-scatter.13
  806.0 44.4 reduce-scatter.11
  904.4 33.0 reduce-scatter.19
  939.8 33.0 reduce-scatter.17
  977.3 67.5 reduce-scatter.15
  1048.7 66.7 reduce-scatter.27
  1119.9 66.8 reduce-scatter.23
  1190.7 148.0 reduce-scatter.29
  1342.5 148.0 reduce-scatter.31
  1495.0 73.3 reduce-scatter.21
  1572.4 117.1 reduce-scatter.25
  1696.7 122.1 all-reduce.6
  1820.5 17.6 all-gather.29
  1841.0 80.0 all-reduce.8
